TPU v7x, 256 devices: a whole 4x4x8 slice. The times are simulated.
256 devices in a mesh: comp: 4 (over y), gx: 16 (over z_hi, x), gy: 4 (over z_lo, core).
Axes of the slice: x: 4, y: 4, z: 8 (z_hi: 4, z_lo: 2; z = z_hi * 2 + z_lo), core: 2. Of those that a mesh axis runs over, the one named last changes fastest.
Arguments:
- state: float32 [32, 256, 128, 128], P('comp', 'gx', 'gy'), may hold values from -4 to 4
- levels: int32 [256, 128], P('gx', 'gy'), may hold values from 0 to 128
- reaction: float32 [3, 8, 8], replicated, may hold values from -2 to 2
Outputs:
- new_state: float32 [32, 256, 128, 128], P('comp', 'gx', 'gy')
Inputs may be any that keep to these rules, and one draw needn't show every extreme that they name: `levels`: 0 marks a land column, 128 a column of full depth.
All inputs are finite; a program needn't handle non-finite values.
Results may differ from a plain program's by a relative error of at most 0.00018.
Values sent between devices are 32-bit elements; how exact they have to be, the bound alone decides.
A program may use at most 64 MiB of HBM per device.

v0:
```python
import jax
import jax.numpy as jnp
from jax import lax
from jax.sharding import PartitionSpec as P

ITERS = 3


time_step = 0.25
lateral_mix = 0.05
vertical_mix = 0.1
pressure_scale = 0.05
thermal_coef = 1.0
haline_coef = 0.8
coriolis_mean = 0.5
coriolis_slope = 0.5


def padded_2(cells, sides, width):
    for axis, dim in sides:
        count = lax.axis_size(axis)
        head = lax.slice_in_dim(cells, 0, width, axis=dim)
        tail = lax.slice_in_dim(cells, cells.shape[dim] - width, cells.shape[dim], axis=dim)
        cells = jnp.concatenate(
            [
                lax.ppermute(tail, axis, [(i, (i + 1) % count) for i in range(count)]),
                cells,
                lax.ppermute(head, axis, [((i + 1) % count, i) for i in range(count)]),
            ],
            axis=dim,
        )
    return cells


def padded_to(lines, length):
    spare = -lines.shape[0] % length
    if not spare:
        return lines
    return jnp.concatenate([lines, jnp.zeros((spare, *lines.shape[1:]), lines.dtype)])


def from_root(value, axis, root):
    lines = jnp.where(lax.axis_index(axis) == root, value, jnp.zeros_like(value)).reshape(
        -1, *value.shape[1:][-1:]
    )
    padded = padded_to(lines, lax.axis_size(axis))
    own = lax.psum_scatter(padded, axis, scatter_dimension=0, tiled=True)
    return lax.all_gather(own, axis, axis=0, tiled=True)[: len(lines)].reshape(value.shape)


def along(padded, axis, shift):
    count_x = padded.shape[1] - 4
    count_y = padded.shape[2] - 4
    if axis == 1:
        return padded[:, 2 + shift : 2 + shift + count_x, 2 : 2 + count_y]
    return padded[:, 2 : 2 + count_x, 2 + shift : 2 + shift + count_y]


def centered(padded, axis):
    return (
        8.0 * (along(padded, axis, 1) - along(padded, axis, -1))
        - (along(padded, axis, 2) - along(padded, axis, -2))
    ) / 12.0


def smoothing(padded, axis):
    return (
        along(padded, axis, 2)
        + along(padded, axis, -2)
        - 4.0 * (along(padded, axis, 1) + along(padded, axis, -1))
        + 6.0 * along(padded, axis, 0)
    ) / 12.0


def transport(padded, east, north):
    return (
        east * centered(padded, 1)
        + jnp.abs(east) * smoothing(padded, 1)
        + north * centered(padded, 2)
        + jnp.abs(north) * smoothing(padded, 2)
    )


def lateral(padded):
    return (
        along(padded, 1, 1)
        + along(padded, 1, -1)
        + along(padded, 2, 1)
        + along(padded, 2, -1)
        - 4.0 * along(padded, 1, 0)
    )


def vertical(center):
    column = jnp.pad(center, ((0, 0), (0, 0), (0, 0), (1, 1)))
    return column[..., 2:] + column[..., :-2] - 2.0 * center


def dynamics_step(padded, mask, latitude, accumulate):
    center = padded[:, 2:-2, 2:-2]
    east = center[0]
    north = center[1]
    moving = padded[0:4]
    density = haline_coef * padded[3] - thermal_coef * padded[2]
    pressure = (pressure_scale * accumulate(density))[None]
    tendency = (
        lateral_mix * lateral(moving)
        + vertical_mix * vertical(center[0:4])
        - transport(moving, east, north)
    )
    rotation = (coriolis_mean + coriolis_slope * latitude)[None, :, None]
    push_east = tendency[0] + rotation * north - centered(pressure, 1)[0]
    push_north = tendency[1] - rotation * east - centered(pressure, 2)[0]
    tendency = jnp.stack([push_east, push_north, tendency[2], tendency[3]])
    advanced = center[0:4] + time_step * (1.5 * tendency - 0.5 * center[4:8])
    return jnp.concatenate([advanced * mask, tendency * mask])


def tracer_step(padded, velocity, mask, coupling):
    center = padded[:, 2:-2, 2:-2]
    growth = 2.0 * jax.nn.sigmoid(velocity[2])
    reacting = growth * jnp.einsum(
        "ij,jxyz->ixyz", coupling, center, precision=lax.Precision.HIGHEST
    )
    tendency = (
        lateral_mix * lateral(padded)
        + vertical_mix * vertical(center)
        + reacting
        - transport(padded, velocity[0], velocity[1])
    )
    return (center + time_step * tendency) * mask


def per_device(state, levels, reaction):
    cells_y = state.shape[2]
    depth_count = state.shape[3]
    slot = lax.axis_index("comp")
    row_first = lax.axis_index("gy") * cells_y
    total_rows = cells_y * lax.axis_size("gy")
    depth = lax.broadcasted_iota(jnp.int32, (1, 1, depth_count), 2)
    mask = (depth < levels[:, :, None]).astype(jnp.float32)
    lower = lax.broadcasted_iota(jnp.int32, (depth_count, depth_count), 0)
    higher = lax.broadcasted_iota(jnp.int32, (depth_count, depth_count), 1)
    summing = (lower <= higher).astype(jnp.float32)
    coupling = lax.dynamic_index_in_dim(reaction, jnp.maximum(slot - 1, 0), 0, keepdims=False)

    def accumulate(density):
        return jnp.dot(density, summing, precision=lax.Precision.HIGHEST)

    def global_rows(width):
        return row_first - width + lax.iota(jnp.int32, cells_y + 2 * width)

    def latitude(width):
        rows = global_rows(width)
        return 2.0 * rows.astype(jnp.float32) / float(total_rows - 1) - 1.0

    current = state * mask[None]
    for step in range(ITERS):
        extend_padded = padded_2(current, (("gx", 1), ("gy", 2)), 2)
        inside_rows = global_rows(2)
        region_latitude = latitude(0)

        def run_dynamics(operands):
            return dynamics_step(operands[0], operands[2], region_latitude, accumulate)

        def run_tracers(operands):
            return tracer_step(operands[0], operands[1], operands[2], coupling)

        current = lax.cond(
            slot == 0,
            run_dynamics,
            run_tracers,
            (
                extend_padded
                * ((inside_rows >= 0) & (inside_rows < total_rows)).astype(jnp.float32)[
                    None, None, :, None
                ],
                from_root(current[0:3], "comp", 0),
                mask,
            ),
        )
    return current


def solution(mesh):
    in_specs = (P("comp", "gx", "gy", None), P("gx", "gy"), P())
    out_specs = P("comp", "gx", "gy", None)
    return jax.shard_map(
        per_device, mesh=mesh, in_specs=in_specs, out_specs=out_specs, check_vma=False
    )
```

profile of v0, /device:TPU:8, one launch (start us, length us, event | category | flops | bytes accessed | tf_op | source)
XLA Modules:
  0.0 168.2 jit_solution(1472869630248358750)
XLA Ops:
  6.5 0.8 fusion.99
  7.4 1.9 %broadcast_multiply_fusion = f32[8,16,32,128]{3,2,1,0:T(8,128)S(1)} fusion(f32[8,16,32,128]{3,2,1,0:T(8,128)} %param.9, f32[16,32,128]{2,1,0:T(8,128)S(1)} %fusion.99), kind=kLoop, calls=%fused_computation.174 | loop fusion | flops 524288 | bytes 4456448 | tf_op jit(solution)/shard_map/mul | solution.py:157
  9.3 1.1 slice_select_fusion.2
  10.5 1.6 collective-permute-start
  12.1 7.1 %collective-permute-start.1 = (f32[8,2,32,128]{3,2,1,0:T(8,128)S(1)}, f32[8,2,32,128]{3,2,1,0:T(8,128)S(1)}, u32[]{:S(2)}, u32[]{:S(2)}) collective-permute-start(f32[8,2,32,128]{3,2,1,0:T(8,128)S(1)} %get-tuple-element.153), channel_id=1, source_target_pairs={{4,0},{8,4},{12,8},{16,12},{20,16},{24,20},{28,24},{32,28},{36,32}... | collective-permute-start | bytes 786440 | tf_op jit(solution)/shard_map/ppermute | solution.py:28
  19.2 0.6 multiply_add_fusion.3
  19.8 7.6 %collective-permute-done = f32[8,2,32,128]{3,2,1,0:T(8,128)S(1)} collective-permute-done((f32[8,2,32,128]{3,2,1,0:T(8,128)S(1)}, f32[8,2,32,128]{3,2,1,0:T(8,128)S(1)}, u32[]{:S(2)}, u32[]{:S(2)}) %collective-permute-start) | collective-permute-done | bytes 262176 | tf_op jit(solution)/shard_map/ppermute | solution.py:26
  27.4 3.0 %collective-permute-done.1 = f32[8,2,32,128]{3,2,1,0:T(8,128)S(1)} collective-permute-done((f32[8,2,32,128]{3,2,1,0:T(8,128)S(1)}, f32[8,2,32,128]{3,2,1,0:T(8,128)S(1)}, u32[]{:S(2)}, u32[]{:S(2)}) %collective-permute-start.1) | collective-permute-done | bytes 262176 | tf_op jit(solution)/shard_map/ppermute | solution.py:28
  30.6 1.7 %collective-permute-start.3 = (f32[8,20,2,128]{3,2,1,0:T(2,128)S(1)}, f32[8,20,2,128]{3,2,1,0:T(2,128)}, u32[]{:S(2)}, u32[]{:S(2)}) collective-permute-start(f32[8,20,2,128]{3,2,1,0:T(2,128)S(1)} %get-tuple-element.147), channel_id=1, source_target_pairs={{1,0},{2,1},{3,2},{0,3},{5,4},{6,5},{7,6},{4,7},{9,8},{10,9},{11,1... | collective-permute-start | bytes 491528 | tf_op jit(solution)/shard_map/ppermute | solution.py:28
  32.4 0.6 fusion.100
  33.0 2.4 %collective-permute-done.2 = f32[8,20,2,128]{3,2,1,0:T(2,128)S(1)} collective-permute-done((f32[8,20,2,128]{3,2,1,0:T(2,128)S(1)}, f32[8,20,2,128]{3,2,1,0:T(2,128)S(1)}, u32[]{:S(2)}, u32[]{:S(2)}) %collective-permute-start.2) | collective-permute-done | bytes 163872 | tf_op jit(solution)/shard_map/ppermute | solution.py:26
  35.4 0.7 copy-done.8
  36.0 0.2 collective-permute-done.3
  36.3 2.3 %maximum_multiply_fusion = f32[8,20,36,128]{3,2,1,0:T(8,128)S(1)} fusion(f32[8,20,2,128]{3,2,1,0:T(2,128)} %collective-permute-done.3, f32[8,2,32,128]{3,2,1,0:T(8,128)} %copy-done.7, f32[8,16,32,128]{3,2,1,0:T(8,128)} %copy-done.2, f32[8,2,32,128]{3,2,1,0:T(8,128)} %copy-done.6, f32[8,20,2,128]{3,2,1,0:T(2,128)} %copy-done.8, f32[36]{0:T(128)S(1)} %and_convert_fusion), kind=kLoop, calls=%fused_computation.171 | loop fusion | flops 3686400 | bytes 5898384 | tf_op jit(solution)/shard_map/mul | solution.py:174
  38.6 15.0 %all_gather.9 = f32[1536,128]{1,0:T(8,128)S(1)} all-gather(f32[384,128]{1,0:T(8,128)} %reduce-scatter.4.cloned.1.call-done), channel_id=1, replica_groups=mesh['comp'=4,'gx'=16,'gy'=4] {'comp'}, dimensions={0}, use_global_device_ids=true | all-gather | bytes 983040 | tf_op jit(solution)/shard_map/all_gather | solution.py:48
  53.6 8.6 %conditional.3 = (f32[8,16,32,128]{3,2,1,0:T(8,128)S(1)}) conditional(s32[]{:T(128)} %convert_element_type.41, (f32[8,20,36,128]{3,2,1,0:T(8,128)S(1)}, f32[1536,128]{1,0:T(8,128)S(1)}, f32[8,8]{1,0:T(8,128)S(1)}, f32[16,32,128]{2,1,0:T(8,128)S(1)}) %tuple.23, (f32[8,20,36,128]{3,2,1,0:T(8,128)S(1)}, f32[32]{0:T(128)S(1)}, f32[128,128]{1,0:T(8,128)}, ...), branch_computations={%region_1.2_spmd, %region_2.3_spmd} | conditional | flops 155859008 | bytes 41029640 | solution.py:169
  53.6 0.1 divide_multiply_fusion
  53.7 1.7 %copy.9 = f32[8,20,36,128]{3,0,2,1:T(8,128)S(1)} copy(f32[8,20,36,128]{3,2,1,0:T(8,128)S(1)} %get-tuple-element.91) | data formatting | bytes 5898240 | tf_op jit(solution)/shard_map
  55.6 6.1 %fusion.8 = f32[8,16,32,128]{3,0,2,1:T(8,128)S(1)} fusion(f32[8,16,32,128]{3,0,2,1:T(8,128)S(1)} %slice.582, f32[8,20,36,128]{3,0,2,1:T(8,128)S(1)} %copy.9, f32[16,32,128]{2,1,0:T(8,128)S(1)} %get-tuple-element.68, f32[16,32,128]{2,1,0:T(8,128)S(1)} %bitcast.91, f32[16,32,128]{2,1,0:T(8,128)S(1)} %bitcast.93, f32[16,32,128]{2,1,0:T(8,128)S(1)} %bitcast.90, ...), kind=kOutput, calls=%fused_computation.10 | convolution fusion | flops 72351744 | bytes 24645632 | tf_op jit(solution)/shard_map/cond/branch_0_fun/ij,jxyz->ixyz/dot_general | solution.py:122
  61.7 0.4 copy.6
  62.2 1.1 slice_select_fusion.1
  63.5 8.1 %collective-permute-start.5 = (f32[8,2,32,128]{3,2,1,0:T(8,128)S(1)}, f32[8,2,32,128]{3,2,1,0:T(8,128)S(1)}, u32[]{:S(2)}, u32[]{:S(2)}) collective-permute-start(f32[8,2,32,128]{3,2,1,0:T(8,128)S(1)} %get-tuple-element.151), channel_id=1, source_target_pairs={{4,0},{8,4},{12,8},{16,12},{20,16},{24,20},{28,24},{32,28},{36,32}... | collective-permute-start | bytes 786440 | tf_op jit(solution)/shard_map/ppermute | solution.py:28
  71.6 8.9 %collective-permute-done.4 = f32[8,2,32,128]{3,2,1,0:T(8,128)S(1)} collective-permute-done((f32[8,2,32,128]{3,2,1,0:T(8,128)S(1)}, f32[8,2,32,128]{3,2,1,0:T(8,128)S(1)}, u32[]{:S(2)}, u32[]{:S(2)}) %collective-permute-start.4) | collective-permute-done | bytes 262176 | tf_op jit(solution)/shard_map/ppermute | solution.py:26
  80.7 1.7 %collective-permute-start.7 = (f32[8,20,2,128]{3,2,1,0:T(2,128)S(1)}, f32[8,20,2,128]{3,2,1,0:T(2,128)S(1)}, u32[]{:S(2)}, u32[]{:S(2)}) collective-permute-start(f32[8,20,2,128]{3,2,1,0:T(2,128)S(1)} %get-tuple-element.145), channel_id=1, source_target_pairs={{1,0},{2,1},{3,2},{0,3},{5,4},{6,5},{7,6},{4,7},{9,8},{10,9},{11,1... | collective-permute-start | bytes 491528 | tf_op jit(solution)/shard_map/ppermute | solution.py:28
  82.5 4.4 %collective-permute-done.6 = f32[8,20,2,128]{3,2,1,0:T(2,128)S(1)} collective-permute-done((f32[8,20,2,128]{3,2,1,0:T(2,128)S(1)}, f32[8,20,2,128]{3,2,1,0:T(2,128)S(1)}, u32[]{:S(2)}, u32[]{:S(2)}) %collective-permute-start.6) | collective-permute-done | bytes 163872 | tf_op jit(solution)/shard_map/ppermute | solution.py:26
  86.9 2.1 %maximum_multiply_fusion.1 = f32[8,20,36,128]{3,2,1,0:T(8,128)S(1)} fusion(f32[8,20,2,128]{3,2,1,0:T(2,128)S(1)} %collective-permute-done.7, f32[8,2,32,128]{3,2,1,0:T(8,128)S(1)} %collective-permute-done.5, f32[8,16,32,128]{3,2,1,0:T(8,128)} %copy-done.3, f32[8,2,32,128]{3,2,1,0:T(8,128)S(1)} %collective-permute-done.4, ...), kind=kLoop, calls=%fused_computation.172 | loop fusion | flops 3686400 | bytes 5898384 | tf_op jit(solution)/shard_map/mul | solution.py:174
  89.0 14.8 %all_gather.10 = f32[1536,128]{1,0:T(8,128)S(1)} all-gather(f32[384,128]{1,0:T(8,128)} %reduce-scatter.6.cloned.1.call-done), channel_id=1, replica_groups=mesh['comp'=4,'gx'=16,'gy'=4] {'comp'}, dimensions={0}, use_global_device_ids=true | all-gather | bytes 983040 | tf_op jit(solution)/shard_map/all_gather | solution.py:48
  103.8 8.6 %conditional.4 = (f32[8,16,32,128]{3,2,1,0:T(8,128)S(1)}) conditional(s32[]{:T(128)} %convert_element_type.41, (f32[8,20,36,128]{3,2,1,0:T(8,128)S(1)}, f32[1536,128]{1,0:T(8,128)S(1)}, f32[8,8]{1,0:T(8,128)S(1)}, f32[16,32,128]{2,1,0:T(8,128)S(1)}) %tuple.25, (f32[8,20,36,128]{3,2,1,0:T(8,128)S(1)}, f32[32]{0:T(128)S(1)}, f32[128,128]{1,0:T(8,128)}, ...), branch_computations={%region_4.5_spmd, %region_5.6_spmd} | conditional | flops 155859008 | bytes 41029640 | solution.py:169
  103.8 0.1 divide_multiply_fusion.1
  104.0 1.7 %copy.10 = f32[8,20,36,128]{3,0,2,1:T(8,128)S(1)} copy(f32[8,20,36,128]{3,2,1,0:T(8,128)S(1)} %get-tuple-element.95) | data formatting | bytes 5898240 | tf_op jit(solution)/shard_map
  105.8 6.1 %fusion.41 = f32[8,16,32,128]{3,0,2,1:T(8,128)S(1)} fusion(f32[8,16,32,128]{3,0,2,1:T(8,128)S(1)} %slice.602, f32[8,20,36,128]{3,0,2,1:T(8,128)S(1)} %copy.10, f32[16,32,128]{2,1,0:T(8,128)S(1)} %get-tuple-element.76, f32[16,32,128]{2,1,0:T(8,128)S(1)} %bitcast.96, f32[16,32,128]{2,1,0:T(8,128)S(1)} %bitcast.98, f32[16,32,128]{2,1,0:T(8,128)S(1)} %bitcast.95, ...), kind=kOutput, calls=%fused_computation.67 | convolution fusion | flops 72351744 | bytes 24645632 | tf_op jit(solution)/shard_map/cond/branch_0_fun/ij,jxyz->ixyz/dot_general | solution.py:122
  112.0 0.4 copy.7
  112.4 1.1 slice_select_fusion
  113.7 6.2 %collective-permute-start.9 = (f32[8,2,32,128]{3,2,1,0:T(8,128)S(1)}, f32[8,2,32,128]{3,2,1,0:T(8,128)S(1)}, u32[]{:S(2)}, u32[]{:S(2)}) collective-permute-start(f32[8,2,32,128]{3,2,1,0:T(8,128)S(1)} %get-tuple-element.149), channel_id=1, source_target_pairs={{4,0},{8,4},{12,8},{16,12},{20,16},{24,20},{28,24},{32,28},{36,32}... | collective-permute-start | bytes 786440 | tf_op jit(solution)/shard_map/ppermute | solution.py:28
  119.9 5.9 %collective-permute-done.8 = f32[8,2,32,128]{3,2,1,0:T(8,128)S(1)} collective-permute-done((f32[8,2,32,128]{3,2,1,0:T(8,128)S(1)}, f32[8,2,32,128]{3,2,1,0:T(8,128)S(1)}, u32[]{:S(2)}, u32[]{:S(2)}) %collective-permute-start.8) | collective-permute-done | bytes 262176 | tf_op jit(solution)/shard_map/ppermute | solution.py:26
  125.8 1.4 collective-permute-done.9
  127.5 2.4 %collective-permute-start.11 = (f32[8,20,2,128]{3,2,1,0:T(2,128)S(1)}, f32[8,20,2,128]{3,2,1,0:T(2,128)S(1)}, u32[]{:S(2)}, u32[]{:S(2)}) collective-permute-start(f32[8,20,2,128]{3,2,1,0:T(2,128)S(1)} %get-tuple-element.143), channel_id=1, source_target_pairs={{1,0},{2,1},{3,2},{0,3},{5,4},{6,5},{7,6},{4,7},{9,8},{10,9},{11,1... | collective-permute-start | bytes 491528 | tf_op jit(solution)/shard_map/ppermute | solution.py:28
  129.8 2.9 %collective-permute-done.10 = f32[8,20,2,128]{3,2,1,0:T(2,128)S(1)} collective-permute-done((f32[8,20,2,128]{3,2,1,0:T(2,128)S(1)}, f32[8,20,2,128]{3,2,1,0:T(2,128)S(1)}, u32[]{:S(2)}, u32[]{:S(2)}) %collective-permute-start.10) | collective-permute-done | bytes 163872 | tf_op jit(solution)/shard_map/ppermute | solution.py:26
  132.8 1.2 collective-permute-done.11
  134.0 2.1 %maximum_multiply_fusion.2 = f32[8,20,36,128]{3,2,1,0:T(8,128)S(1)} fusion(f32[8,20,2,128]{3,2,1,0:T(2,128)S(1)} %collective-permute-done.11, f32[8,2,32,128]{3,2,1,0:T(8,128)S(1)} %collective-permute-done.9, f32[8,16,32,128]{3,2,1,0:T(8,128)} %copy-done.4, f32[8,2,32,128]{3,2,1,0:T(8,128)S(1)} %collective-permute-done.8, ...), kind=kLoop, calls=%fused_computation.173 | loop fusion | flops 3686400 | bytes 5898384 | tf_op jit(solution)/shard_map/mul | solution.py:174
  136.1 0.6 reduce-scatter.8.cloned.1.call-done
  136.7 14.4 %all_gather.11 = f32[1536,128]{1,0:T(8,128)S(1)} all-gather(f32[384,128]{1,0:T(8,128)} %reduce-scatter.8.cloned.1.call-done), channel_id=1, replica_groups=mesh['comp'=4,'gx'=16,'gy'=4] {'comp'}, dimensions={0}, use_global_device_ids=true | all-gather | bytes 983040 | tf_op jit(solution)/shard_map/all_gather | solution.py:48
  151.1 8.6 %conditional.5 = (f32[8,16,32,128]{3,2,1,0:T(8,128)S(1)}) conditional(s32[]{:T(128)} %convert_element_type.41, (f32[8,20,36,128]{3,2,1,0:T(8,128)S(1)}, f32[1536,128]{1,0:T(8,128)S(1)}, f32[8,8]{1,0:T(8,128)S(1)}, f32[16,32,128]{2,1,0:T(8,128)S(1)}) %tuple.27, (f32[8,20,36,128]{3,2,1,0:T(8,128)S(1)}, f32[32]{0:T(128)S(1)}, f32[128,128]{1,0:T(8,128)}, ...), branch_computations={%region_7.8_spmd, %region_8.9_spmd} | conditional | flops 155859008 | bytes 41029640 | solution.py:169
  151.2 1.7 %copy.11 = f32[8,20,36,128]{3,0,2,1:T(8,128)S(1)} copy(f32[8,20,36,128]{3,2,1,0:T(8,128)S(1)} %get-tuple-element.99) | data formatting | bytes 5898240 | tf_op jit(solution)/shard_map
  153.1 6.1 %fusion.74 = f32[8,16,32,128]{3,0,2,1:T(8,128)S(1)} fusion(f32[8,16,32,128]{3,0,2,1:T(8,128)S(1)} %slice.622, f32[8,20,36,128]{3,0,2,1:T(8,128)S(1)} %copy.11, f32[16,32,128]{2,1,0:T(8,128)S(1)} %get-tuple-element.84, f32[16,32,128]{2,1,0:T(8,128)S(1)} %bitcast.101, f32[16,32,128]{2,1,0:T(8,128)S(1)} %bitcast.103, f32[16,32,128]{2,1,0:T(8,128)S(1)} %bitcast.100, ...), kind=kOutput, calls=%fused_computation.124 | convolution fusion | flops 72351744 | bytes 24645632 | tf_op jit(solution)/shard_map/cond/branch_0_fun/ij,jxyz->ixyz/dot_general | solution.py:122
  159.2 0.4 copy.8
  159.7 1.3 copy-done.5
  161.0 0.7 copy-done.1
  (44 shorter events, 1.7 us)
Async XLA Ops:
  6.5 13.3 %copy-start = (f32[3,8,8]{2,1,0:T(8,128)S(1)}, f32[3,8,8]{2,1,0:T(8,128)}, u32[]{:S(2)}) copy-start(f32[3,8,8]{2,1,0:T(8,128)} %param.11) | copy-start | bytes 2308
  6.5 32.0 %reduce-scatter.4.cloned.1.call-start = ((), (), s32[]{:S(2)}) async-start(), calls=%async_computation.3 | async-start | bytes 983040 | tf_op jit(solution)/shard_map/reduce_scatter | solution.py:47
  9.3 21.2 %copy-start.2 = (f32[8,16,32,128]{3,2,1,0:T(8,128)}, f32[8,16,32,128]{3,2,1,0:T(8,128)S(1)}, u32[]{:S(2)}) copy-start(f32[8,16,32,128]{3,2,1,0:T(8,128)S(1)} %broadcast_multiply_fusion) | copy-start | bytes 6291460
  10.4 78.6 %reduce-scatter.6.cloned.1.call-start = ((), (), s32[]{:S(2)}) async-start(), calls=%async_computation.4 | async-start | bytes 983040 | tf_op jit(solution)/shard_map/reduce_scatter | solution.py:47
  10.5 16.9 %collective-permute-start = (f32[8,2,32,128]{3,2,1,0:T(8,128)S(1)}, f32[8,2,32,128]{3,2,1,0:T(8,128)S(1)}, u32[]{:S(2)}, u32[]{:S(2)}) collective-permute-start(f32[8,2,32,128]{3,2,1,0:T(8,128)S(1)} %get-tuple-element.152), channel_id=1, source_target_pairs={{0,4},{4,8},{8,12},{12,16},{16,20},{20,24},{24,28},{28,32},{32,36}... | collective-permute-start | bytes 786440 | tf_op jit(solution)/shard_map/ppermute | solution.py:26
  12.1 18.3 %collective-permute-start.1 = (f32[8,2,32,128]{3,2,1,0:T(8,128)S(1)}, f32[8,2,32,128]{3,2,1,0:T(8,128)S(1)}, u32[]{:S(2)}, u32[]{:S(2)}) collective-permute-start(f32[8,2,32,128]{3,2,1,0:T(8,128)S(1)} %get-tuple-element.153), channel_id=1, source_target_pairs={{4,0},{8,4},{12,8},{16,12},{20,16},{24,20},{28,24},{32,28},{36,32}... | collective-permute-start | bytes 786440 | tf_op jit(solution)/shard_map/ppermute | solution.py:28
  27.4 8.0 %copy-start.6 = (f32[8,2,32,128]{3,2,1,0:T(8,128)}, f32[8,2,32,128]{3,2,1,0:T(8,128)S(1)}, u32[]{:S(2)}) copy-start(f32[8,2,32,128]{3,2,1,0:T(8,128)S(1)} %collective-permute-done) | copy-start | bytes 786436
  30.4 5.0 %copy-start.7 = (f32[8,2,32,128]{3,2,1,0:T(8,128)}, f32[8,2,32,128]{3,2,1,0:T(8,128)S(1)}, u32[]{:S(2)}) copy-start(f32[8,2,32,128]{3,2,1,0:T(8,128)S(1)} %collective-permute-done.1) | copy-start | bytes 786436
  30.5 4.8 %collective-permute-start.2 = (f32[8,20,2,128]{3,2,1,0:T(2,128)S(1)}, f32[8,20,2,128]{3,2,1,0:T(2,128)S(1)}, u32[]{:S(2)}, u32[]{:S(2)}) collective-permute-start(f32[8,20,2,128]{3,2,1,0:T(2,128)S(1)} %get-tuple-element.146), channel_id=1, source_target_pairs={{0,1},{1,2},{2,3},{3,0},{4,5},{5,6},{6,7},{7,4},{8,9},{9,10},{10,1... | collective-permute-start | bytes 491528 | tf_op jit(solution)/shard_map/ppermute | solution.py:26
  30.6 5.6 %collective-permute-start.3 = (f32[8,20,2,128]{3,2,1,0:T(2,128)S(1)}, f32[8,20,2,128]{3,2,1,0:T(2,128)}, u32[]{:S(2)}, u32[]{:S(2)}) collective-permute-start(f32[8,20,2,128]{3,2,1,0:T(2,128)S(1)} %get-tuple-element.147), channel_id=1, source_target_pairs={{1,0},{2,1},{3,2},{0,3},{5,4},{6,5},{7,6},{4,7},{9,8},{10,9},{11,1... | collective-permute-start | bytes 491528 | tf_op jit(solution)/shard_map/ppermute | solution.py:28
  33.0 20.6 %copy-start.9 = (f32[32]{0:T(128)S(1)}, f32[32]{0:T(128)}, u32[]{:S(2)}) copy-start(f32[32]{0:T(128)} %multiply_add_fusion.3) | copy-start | bytes 388
  35.4 0.7 copy-start.8
  62.2 18.5 %copy-start.3 = (f32[8,16,32,128]{3,2,1,0:T(8,128)}, f32[8,16,32,128]{3,2,1,0:T(8,128)S(1)}, u32[]{:S(2)}) copy-start(f32[8,16,32,128]{3,2,1,0:T(8,128)S(1)} %get-tuple-element.156) | copy-start | bytes 6291460
  63.3 73.4 %reduce-scatter.8.cloned.1.call-start = ((), (), s32[]{:S(2)}) async-start(), calls=%async_computation.5 | async-start | bytes 983040 | tf_op jit(solution)/shard_map/reduce_scatter | solution.py:47
  63.4 17.1 %collective-permute-start.4 = (f32[8,2,32,128]{3,2,1,0:T(8,128)S(1)}, f32[8,2,32,128]{3,2,1,0:T(8,128)S(1)}, u32[]{:S(2)}, u32[]{:S(2)}) collective-permute-start(f32[8,2,32,128]{3,2,1,0:T(8,128)S(1)} %get-tuple-element.150), channel_id=1, source_target_pairs={{0,4},{4,8},{8,12},{12,16},{16,20},{20,24},{24,28},{28,32},{32,36}... | collective-permute-start | bytes 786440 | tf_op jit(solution)/shard_map/ppermute | solution.py:26
  63.5 17.1 %collective-permute-start.5 = (f32[8,2,32,128]{3,2,1,0:T(8,128)S(1)}, f32[8,2,32,128]{3,2,1,0:T(8,128)S(1)}, u32[]{:S(2)}, u32[]{:S(2)}) collective-permute-start(f32[8,2,32,128]{3,2,1,0:T(8,128)S(1)} %get-tuple-element.151), channel_id=1, source_target_pairs={{4,0},{8,4},{12,8},{16,12},{20,16},{24,20},{28,24},{32,28},{36,32}... | collective-permute-start | bytes 786440 | tf_op jit(solution)/shard_map/ppermute | solution.py:28
  80.7 6.2 %collective-permute-start.6 = (f32[8,20,2,128]{3,2,1,0:T(2,128)S(1)}, f32[8,20,2,128]{3,2,1,0:T(2,128)S(1)}, u32[]{:S(2)}, u32[]{:S(2)}) collective-permute-start(f32[8,20,2,128]{3,2,1,0:T(2,128)S(1)} %get-tuple-element.144), channel_id=1, source_target_pairs={{0,1},{1,2},{2,3},{3,0},{4,5},{5,6},{6,7},{7,4},{8,9},{9,10},{10,1... | collective-permute-start | bytes 491528 | tf_op jit(solution)/shard_map/ppermute | solution.py:26
  80.7 6.1 %collective-permute-start.7 = (f32[8,20,2,128]{3,2,1,0:T(2,128)S(1)}, f32[8,20,2,128]{3,2,1,0:T(2,128)S(1)}, u32[]{:S(2)}, u32[]{:S(2)}) collective-permute-start(f32[8,20,2,128]{3,2,1,0:T(2,128)S(1)} %get-tuple-element.145), channel_id=1, source_target_pairs={{1,0},{2,1},{3,2},{0,3},{5,4},{6,5},{7,6},{4,7},{9,8},{10,9},{11,1... | collective-permute-start | bytes 491528 | tf_op jit(solution)/shard_map/ppermute | solution.py:28
  112.4 15.0 %copy-start.4 = (f32[8,16,32,128]{3,2,1,0:T(8,128)}, f32[8,16,32,128]{3,2,1,0:T(8,128)S(1)}, u32[]{:S(2)}) copy-start(f32[8,16,32,128]{3,2,1,0:T(8,128)S(1)} %get-tuple-element.157) | copy-start | bytes 6291460
  113.6 12.2 %collective-permute-start.8 = (f32[8,2,32,128]{3,2,1,0:T(8,128)S(1)}, f32[8,2,32,128]{3,2,1,0:T(8,128)S(1)}, u32[]{:S(2)}, u32[]{:S(2)}) collective-permute-start(f32[8,2,32,128]{3,2,1,0:T(8,128)S(1)} %get-tuple-element.148), channel_id=1, source_target_pairs={{0,4},{4,8},{8,12},{12,16},{16,20},{20,24},{24,28},{28,32},{32,36}... | collective-permute-start | bytes 786440 | tf_op jit(solution)/shard_map/ppermute | solution.py:26
  113.7 13.6 %collective-permute-start.9 = (f32[8,2,32,128]{3,2,1,0:T(8,128)S(1)}, f32[8,2,32,128]{3,2,1,0:T(8,128)S(1)}, u32[]{:S(2)}, u32[]{:S(2)}) collective-permute-start(f32[8,2,32,128]{3,2,1,0:T(8,128)S(1)} %get-tuple-element.149), channel_id=1, source_target_pairs={{4,0},{8,4},{12,8},{16,12},{20,16},{24,20},{28,24},{32,28},{36,32}... | collective-permute-start | bytes 786440 | tf_op jit(solution)/shard_map/ppermute | solution.py:28
  127.4 5.4 %collective-permute-start.10 = (f32[8,20,2,128]{3,2,1,0:T(2,128)S(1)}, f32[8,20,2,128]{3,2,1,0:T(2,128)S(1)}, u32[]{:S(2)}, u32[]{:S(2)}) collective-permute-start(f32[8,20,2,128]{3,2,1,0:T(2,128)S(1)} %get-tuple-element.142), channel_id=1, source_target_pairs={{0,1},{1,2},{2,3},{3,0},{4,5},{5,6},{6,7},{7,4},{8,9},{9,10},{10,1... | collective-permute-start | bytes 491528 | tf_op jit(solution)/shard_map/ppermute | solution.py:26
  127.5 6.5 %collective-permute-start.11 = (f32[8,20,2,128]{3,2,1,0:T(2,128)S(1)}, f32[8,20,2,128]{3,2,1,0:T(2,128)S(1)}, u32[]{:S(2)}, u32[]{:S(2)}) collective-permute-start(f32[8,20,2,128]{3,2,1,0:T(2,128)S(1)} %get-tuple-element.143), channel_id=1, source_target_pairs={{1,0},{2,1},{3,2},{0,3},{5,4},{6,5},{7,6},{4,7},{9,8},{10,9},{11,1... | collective-permute-start | bytes 491528 | tf_op jit(solution)/shard_map/ppermute | solution.py:28
  159.7 1.3 copy-start.5
  161.0 0.7 copy-start.1
Sparse Core Ops, SparseCore 0:
  10.6 25.7 reduce-scatter.3
  63.4 24.0 reduce-scatter.5
  113.6 22.9 reduce-scatter.7
where the time goes:
time: 170 us; the launch traced here: 168 us
  blocking collectives  44.2 us (26%)
  waiting for transfers between devices  38.7 us (23%)
  starting transfers between devices  29.3 us (17%)
  matrix products  18.4 us (11%)
  other arithmetic  14.5 us (9%)
  between operations  13.3 us (8%)
  local copies, waits for them, and re-layouts  9.62 us (6%)
    all_gather x3, blocking collectives, from_root(): lax.all_gather(own, axis, axis=0, tiled=True)[:len(lines)]  44.2 us
    ppermute x6, waiting for transfers between devices, padded_2(): lax.ppermute(tail, axis, [(i, (i + 1) % count) for i in range(count)])  32.2 us
    ppermute x6, starting transfers between devices, padded_2(): lax.ppermute(head, axis, [((i + 1) % count, i) for i in range(count)])  27.3 us
    dot_general x3, matrix products, tracer_step(): jnp.einsum('ij,jxyz->ixyz', coupling, center, precision=lax.Precision.HIG...  18.4 us
    mul x3, other arithmetic, per_device(): extend_padded * ((inside_rows >= 0) & (inside_rows < total_rows)).astype(...  6.49 us
    ppermute x6, waiting for transfers between devices, padded_2(): lax.ppermute(head, axis, [((i + 1) % count, i) for i in range(count)])  5.92 us
    another operation x3, local copies, waits for them, and re-layouts  5.13 us
  transfers between devices with their start and end apart: 15, of which 11 were waited for; matrix products, arithmetic and copies ran while one was open for 5% of the time, Pallas kernels for 0%

commit v1 on v0

v1 whole, which is shorter than its diff:
```python
import functools

import jax
import jax.numpy as jnp
from jax import lax
from jax.experimental import pallas as pl
from jax.experimental.pallas import tpu as pltpu
from jax.sharding import PartitionSpec as P

MESH = pl.DeviceIdType.MESH
ITERS = 3
EDGE = 8
X_CHIPS = 4
LAG = 4

time_step = 0.25
lateral_mix = 0.05
vertical_mix = 0.1
pressure_scale = 0.05
thermal_coef = 1.0
haline_coef = 0.8
coriolis_mean = 0.5
coriolis_slope = 0.5


def weights(speed, scale):
    size = jnp.abs(speed)
    mix = scale * lateral_mix
    eight = speed * (scale * 8.0 / 12.0)
    four = size * (scale * 4.0 / 12.0) + mix
    return four - eight, four + eight, (speed - size) * (scale / 12.0), (speed + size) * (-scale / 12.0)


def kernel(
    mesh_size, state_ref, levels_ref, reaction_ref, out_ref, pad, vel, mask, mixing, summing, slope, push,
    load_sem, out_sem, vel_send, vel_recv, x_send, x_recv, y_send, y_recv,
):
    count_gx, count_gy = mesh_size
    fields, rows, cells_y, depth = state_ref.shape
    pairs = rows // 2
    tiles = cells_y // 8
    slot = lax.axis_index("comp")
    gx = lax.axis_index("gx")
    gy = lax.axis_index("gy")
    east = lax.rem(gx + 1, count_gx)
    west = lax.rem(gx + count_gx - 1, count_gx)
    south = lax.rem(gy + 1, count_gy)
    north = lax.rem(gy + count_gy - 1, count_gy)
    inside = pl.ds(EDGE, cells_y)

    def load(j, first, size):
        return pltpu.make_async_copy(
            state_ref.at[:, pl.ds(first, size)], pad.at[0, :, pl.ds(2 + first, size), inside], load_sem.at[j]
        )

    loads = [load(0, 0, 2), load(1, rows - 2, 2), load(2, 2, rows - 4)]
    for copy in loads:
        copy.start()

    barrier = pltpu.get_barrier_semaphore()
    for near in (
        {"gx": east}, {"gx": west}, {"gy": south}, {"gy": north},
        {"comp": lax.rem(slot + 1, 4)}, {"comp": lax.rem(slot + 3, 4)},
    ):
        pl.semaphore_signal(barrier, inc=1, device_id=near, device_id_type=MESH)

    lane = lax.broadcasted_iota(jnp.int32, (8, depth), 1)
    own_y = lax.broadcasted_iota(jnp.int32, (8, cells_y), 0)
    at_y = lax.broadcasted_iota(jnp.int32, (8, cells_y), 1)
    lanes = lane.astype(jnp.float32)
    for row in range(rows):
        level = jnp.broadcast_to(levels_ref[pl.ds(row, 1), :], (8, cells_y)).astype(jnp.float32)
        for t in range(tiles):
            column = jnp.sum(jnp.where(at_y == own_y + 8 * t, level, 0.0), axis=1, keepdims=True)
            mask[row, pl.ds(8 * t, 8)] = jnp.where(lanes < column, 1.0, 0.0)

    def wall(first):
        zeros = jnp.zeros((8, depth), jnp.float32)

        @pl.loop(0, rows)
        def _(row):
            for step in range(ITERS):
                for f in range(fields):
                    pad[step, f, 2 + row, pl.ds(first, 8)] = zeros

    pl.when(gy == 0)(lambda: wall(0))
    pl.when(gy == count_gy - 1)(lambda: wall(EDGE + cells_y))

    up = jnp.where(lane > 0, 1.0, 0.0)
    down = jnp.where(lane < depth - 1, 1.0, 0.0)

    def cover(row):
        for f in range(fields):
            pad[0, f, 2 + row, inside] = pad[0, f, 2 + row, inside] * mask[row]

    def send_x(step, j, kinds):
        for side, row, to_row, to in ((0, j, rows + j, west), (1, rows - 1 - j, -1 - j, east)):
            pltpu.make_async_remote_copy(
                src_ref=pad.at[step, pl.ds(0, kinds), 2 + row, inside],
                dst_ref=pad.at[step, pl.ds(0, kinds), 2 + to_row, inside],
                send_sem=x_send.at[step, side, j],
                recv_sem=x_recv.at[step, side, j],
                device_id={"gx": to},
                device_id_type=MESH,
            ).start()

    def end_x(step, j, kinds, sent):
        for side in range(2):
            block = pad.at[step, pl.ds(0, kinds), 2, inside]
            copy = pltpu.make_async_remote_copy(
                src_ref=block, dst_ref=block, send_sem=x_send.at[step, side, j], recv_sem=x_recv.at[step, side, j],
                device_id={"gx": east}, device_id_type=MESH,
            )
            copy.wait_send() if sent else copy.wait_recv()

    def y_copies(step, j, kinds):
        for group in (j, pairs - 1 - j):
            for side, first, to_first, to in ((0, EDGE, EDGE + cells_y, north), (1, EDGE + cells_y - 2, EDGE - 2, south)):
                yield side, pltpu.make_async_remote_copy(
                    src_ref=pad.at[step, pl.ds(0, kinds), pl.ds(2 + 2 * group, 2), pl.ds(first, 2)],
                    dst_ref=pad.at[step, pl.ds(0, kinds), pl.ds(2 + 2 * group, 2), pl.ds(to_first, 2)],
                    send_sem=y_send.at[step, side, group],
                    recv_sem=y_recv.at[step, side, group],
                    device_id={"gy": to},
                    device_id_type=MESH,
                )

    def send_y(step, j, kinds):
        for side, copy in y_copies(step, j, kinds):
            pl.when(gy > 0 if side == 0 else gy < count_gy - 1)(copy.start)

    def end_y(step, j, kinds, sent):
        for side, copy in y_copies(step, j, kinds):
            if sent:
                pl.when(gy > 0 if side == 0 else gy < count_gy - 1)(copy.wait_send)
            else:
                pl.when(gy < count_gy - 1 if side == 0 else gy > 0)(copy.wait_recv)

    def write(j):
        for group in (j, pairs - 1 - j):
            yield pltpu.make_async_copy(
                pad.at[ITERS, :, pl.ds(2 + 2 * group, 2), inside], out_ref.at[:, pl.ds(2 * group, 2)], out_sem.at[group]
            )

    def vel_copy(step, row, source, to):
        return pltpu.make_async_remote_copy(
            src_ref=source,
            dst_ref=vel.at[step, :, row],
            send_sem=vel_send.at[step, row],
            recv_sem=vel_recv.at[step, row],
            device_id={"comp": to},
            device_id_type=MESH,
        )

    def send_vel(step, k):
        for row, to in ((k, 1), (rows - 1 - k, 3)):
            vel_copy(step, row, pad.at[step, pl.ds(0, 3), 2 + row, inside], to).start()

    def start(kinds, feeds):
        for j in range(2):
            loads[j].wait()
        for row in (0, rows - 1, 1, rows - 2):
            cover(row)
        pl.semaphore_wait(barrier, 6)
        for j in range(2):
            if feeds:
                send_vel(0, j)
            send_x(0, j, kinds)
        send_y(0, 0, kinds)
        loads[2].wait()

        @pl.loop(1, pairs // 2)
        def _(j):
            for k in (2 * j, 2 * j + 1):
                cover(k)
                cover(rows - 1 - k)
            if feeds:
                send_vel(0, 2 * j)
                send_vel(0, 2 * j + 1)
            send_y(0, j, kinds)

    def each_pair(kinds, compute, after):
        @pl.loop(0, ITERS * pairs)
        def _(n):
            step = n // pairs
            k = n % pairs
            odd = k % 2

            @pl.when(k == 0)
            def _():
                for j in range(2):
                    end_x(step, j, kinds, False)

            @pl.when(odd == 0)
            def _():
                end_y(step, k // 2, kinds, False)

            compute(n, step, k)

            @pl.when(step < ITERS - 1)
            def _():
                after(step + 1, k)

                @pl.when(k < 2)
                def _():
                    send_x(step + 1, k, kinds)

                @pl.when(odd == 1)
                def _():
                    send_y(step + 1, k // 2, kinds)

            @pl.when((step == ITERS - 1) & (odd == 1))
            def _():
                for copy in write(k // 2):
                    copy.start()

        @pl.loop(0, ITERS)
        def _(step):
            for j in range(2):
                end_x(step, j, kinds, True)

            @pl.loop(0, pairs // 2)
            def _(j):
                end_y(step, j, kinds, True)

        for j in range(pairs // 2):
            for copy in write(j):
                copy.wait()

    def turn(q, by):
        return pltpu.roll(q, by % depth, 1)

    def cell(step, f, x, t, shift=0):
        return pad[step, f, x, pl.ds(EDGE + 8 * t + shift, 8)]

    def density_slopes(step, row, at):
        x = row + 2
        scale = pressure_scale / 12.0

        def difference(f, t, along_x):
            if along_x:
                one, two = cell(step, f, x + 1, t) - cell(step, f, x - 1, t), cell(step, f, x + 2, t) - cell(step, f, x - 2, t)
            else:
                one, two = cell(step, f, x, t, 1) - cell(step, f, x, t, -1), cell(step, f, x, t, 2) - cell(step, f, x, t, -2)
            return 8.0 * one - two

        for t in range(tiles):
            for way, along_x in enumerate((True, False)):
                salt, heat = difference(3, t, along_x), difference(2, t, along_x)
                slope[pl.ds(at + (way * tiles + t) * 8, 8)] = (scale * haline_coef) * salt - (scale * thermal_coef) * heat

    def dynamics_row(step, row, at):
        x = row + 2
        for t in range(tiles):
            u, v = cell(step, 0, x, t), cell(step, 1, x, t)
            m = mask[row, pl.ds(8 * t, 8)]
            along_x, along_y = weights(u, 1.0), weights(v, 1.0)
            middle = -0.5 * (jnp.abs(u) + jnp.abs(v)) - (4.0 * lateral_mix + 2.0 * vertical_mix)
            y = gy * cells_y + 8 * t + lax.broadcasted_iota(jnp.int32, (8, depth), 0)
            latitude = 2.0 * y.astype(jnp.float32) / float(cells_y * count_gy - 1) - 1.0
            spin = coriolis_mean + coriolis_slope * latitude
            for f in range(4):
                q = cell(step, f, x, t)
                total = middle * q
                for w, shift in zip(along_x, (1, -1, 2, -2)):
                    total += w * cell(step, f, x + shift, t)
                for w, shift in zip(along_y, (1, -1, 2, -2)):
                    total += w * cell(step, f, x, t, shift)
                total += (vertical_mix * up) * turn(q, 1) + (vertical_mix * down) * turn(q, -1)
                if f == 0:
                    total += spin * v - push[pl.ds(at + t * 8, 8)]
                if f == 1:
                    total -= spin * u + push[pl.ds(at + (tiles + t) * 8, 8)]
                before = cell(step, 4 + f, x, t)
                pad[step + 1, f, x, pl.ds(EDGE + 8 * t, 8)] = m * (
                    q + ((1.5 * time_step) * total - (0.5 * time_step) * before)
                )
                pad[step + 1, 4 + f, x, pl.ds(EDGE + 8 * t, 8)] = m * total

    def run_dynamics():
        above = lax.broadcasted_iota(jnp.int32, (depth, depth), 0)
        below = lax.broadcasted_iota(jnp.int32, (depth, depth), 1)
        summing[...] = jnp.where(above <= below, 1.0, 0.0)
        start(4, True)

        def compute(n, step, k):
            density_slopes(step, k, 0)
            density_slopes(step, rows - 1 - k, 2 * cells_y)
            push[...] = jnp.dot(
                slope[...], summing[...], precision=lax.Precision.HIGHEST, preferred_element_type=jnp.float32
            )
            dynamics_row(step, k, 0)
            dynamics_row(step, rows - 1 - k, 2 * cells_y)

        each_pair(4, compute, send_vel)

        @pl.loop(0, ITERS)
        def _(step):
            @pl.loop(0, rows)
            def _(row):
                vel_copy(step, row, vel.at[step, :, row], 1).wait_send()

    def tracer_row(step, row):
        x = row + 2
        for t0 in range(0, tiles, 2):
            here = []
            for t in (t0, t0 + 1):
                at = pl.ds(8 * t, 8)
                u, v, heat = vel[step, 0, row, at], vel[step, 1, row, at], vel[step, 2, row, at]
                along_x, along_y = weights(u, time_step), weights(v, time_step)
                middle = (-0.5 * time_step) * (jnp.abs(u) + jnp.abs(v)) + (
                    1.0 - time_step * (4.0 * lateral_mix + 2.0 * vertical_mix)
                )
                growth = (2.0 * time_step) * jax.nn.sigmoid(heat)
                q = [cell(step, f, x, t) for f in range(fields)]
                here.append((t, mask[row, at], along_x, along_y, middle, growth, q))
            for f in range(fields):
                rates = [mixing[f, j] for j in range(fields)]
                for t, m, along_x, along_y, middle, growth, q in here:
                    reacting = rates[0] * q[0]
                    for j in range(1, fields):
                        reacting += rates[j] * q[j]
                    total = middle * q[f] + growth * reacting
                    for w, shift in zip(along_x, (1, -1, 2, -2)):
                        total += w * cell(step, f, x + shift, t)
                    for w, shift in zip(along_y, (1, -1, 2, -2)):
                        total += w * cell(step, f, x, t, shift)
                    total += (time_step * vertical_mix * up) * turn(q[f], 1) + (time_step * vertical_mix * down) * turn(q[f], -1)
                    pad[step + 1, f, x, pl.ds(EDGE + 8 * t, 8)] = m * total

    def run_tracers():
        for i in range(fields):
            for j in range(fields):
                mixing[i, j] = jnp.full((8, depth), reaction_ref[slot - 1, i, j], jnp.float32)
        start(fields, False)
        total = ITERS * pairs
        ahead = LAG * (3 - slot) // 2
        behind = LAG * (slot - 1) // 2

        def relay(c, row, last, to):
            copy = vel_copy(c // pairs, row, vel.at[c // pairs, :, row], to)
            copy.wait_recv()
            pl.when(last)(copy.start)

        def going_up(c):
            relay(c, c % pairs, slot < 3, lax.rem(slot + 1, 4))

        def going_down(c):
            relay(c, rows - 1 - c % pairs, slot > 1, slot - 1)

        @pl.loop(0, ahead)
        def _(c):
            going_up(c)

        @pl.loop(0, behind)
        def _(c):
            going_down(c)

        def compute(n, step, k):
            pl.when(n + ahead < total)(lambda: going_up(n + ahead))
            pl.when(n + behind < total)(lambda: going_down(n + behind))
            tracer_row(step, k)
            tracer_row(step, rows - 1 - k)

        each_pair(fields, compute, lambda step, k: None)

        @pl.loop(0, total)
        def _(c):
            step = c // pairs
            k = c % pairs
            pl.when(slot < 3)(lambda: vel_copy(step, k, vel.at[step, :, k], 1).wait_send())
            pl.when(slot > 1)(lambda: vel_copy(step, rows - 1 - k, vel.at[step, :, k], 1).wait_send())

    pl.when(slot == 0)(run_dynamics)
    pl.when(slot != 0)(run_tracers)


def solution(mesh):
    mesh_size = (mesh.shape["gx"], mesh.shape["gy"])

    def per_device(state, levels, reaction):
        fields, rows, cells_y, depth = state.shape
        dma = pltpu.SemaphoreType.DMA
        padded = (fields, rows + 4, cells_y + 2 * EDGE, depth)
        return pl.pallas_call(
            functools.partial(kernel, mesh_size),
            out_shape=jax.ShapeDtypeStruct(state.shape, state.dtype),
            in_specs=[
                pl.BlockSpec(memory_space=pl.ANY),
                pl.BlockSpec(memory_space=pltpu.VMEM),
                pl.BlockSpec(memory_space=pltpu.SMEM),
            ],
            out_specs=pl.BlockSpec(memory_space=pl.ANY),
            scratch_shapes=[
                pltpu.VMEM((ITERS + 1, *padded), jnp.float32),
                pltpu.VMEM((ITERS, 3, rows, cells_y, depth), jnp.float32),
                pltpu.VMEM((rows, cells_y, depth), jnp.float32),
                pltpu.VMEM((fields, fields, 8, depth), jnp.float32),
                pltpu.VMEM((depth, depth), jnp.float32),
                pltpu.VMEM((4 * cells_y, depth), jnp.float32),
                pltpu.VMEM((4 * cells_y, depth), jnp.float32),
                dma((3,)),
                dma((rows // 2,)),
                dma((ITERS, rows)),
                dma((ITERS, rows)),
                dma((ITERS, 2, 2)),
                dma((ITERS, 2, 2)),
                dma((ITERS, 2, rows // 2)),
                dma((ITERS, 2, rows // 2)),
            ],
            compiler_params=pltpu.CompilerParams(
                collective_id=0, has_side_effects=True, vmem_limit_bytes=32 * 1024 * 1024
            ),
        )(state, levels, reaction)

    in_specs = (P("comp", "gx", "gy", None), P("gx", "gy"), P())
    out_specs = P("comp", "gx", "gy", None)
    return jax.shard_map(per_device, mesh=mesh, in_specs=in_specs, out_specs=out_specs, check_vma=False)
```

time: 170 us -> 72.4 us (0.43)
  Pallas kernels: 0 us -> 67.9 us
  blocking collectives: 44.2 us -> 0 us
  waiting for transfers between devices: 38.7 us -> 0 us
  starting transfers between devices: 29.3 us -> 0 us
  matrix products: 18.4 us -> 0 us
  other arithmetic: 14.5 us -> 0 us
  between operations: 13.3 us -> 0.01 us
  local copies, waits for them, and re-layouts: 9.62 us -> 4.31 us
    pallas_call x0 -> x1, Pallas kernels: none -> 67.9 us  [per_device(): pl.pallas_call(functools.partial(kernel, mesh_size), out_shape=jax.ShapeD...]
    all_gather x3 -> x0, blocking collectives: 44.2 us -> none  [from_root(): lax.all_gather(own, axis, axis=0, tiled=True)[:len(lines)]]
    ppermute x12 -> x0, waiting for transfers between devices: 38.1 us -> none  [the longest x6 32.2 us: padded_2(): lax.ppermute(tail, axis, [(i, (i + 1) % count) for i in range(count)])]
    ppermute x12 -> x0, starting transfers between devices: 29.3 us -> none  [the longest x6 27.3 us: padded_2(): lax.ppermute(head, axis, [((i + 1) % count, i) for i in range(count)])]
    dot_general x3 -> x0, matrix products: 18.4 us -> none  [tracer_step(): jnp.einsum('ij,jxyz->ixyz', coupling, center, precision=lax.Precision.HIG...]
    mul x7 -> x0, other arithmetic: 8.85 us -> none  [the longest x3 6.49 us: per_device(): extend_padded * ((inside_rows >= 0) & (inside_rows < total_rows)).astype(...]
    another operation x3 -> x0, local copies, waits for them, and re-layouts: 5.13 us -> none
    select_n x3 -> x0, other arithmetic: 3.24 us -> none  [from_root(): jnp.where(lax.axis_index(axis) == root, value, jnp.zeros_like(value))]
  transfers between devices with their start and end apart: 15 -> 0, of which waited for: 11 -> 0; matrix products, arithmetic and copies ran while one was open for 5% -> 0% of each run, Pallas kernels for 0% -> 0%
where the time goes in v1:
time: 72.4 us; the launch traced here: 72.2 us
  Pallas kernels  67.9 us (94%)
  local copies, waits for them, and re-layouts  4.31 us (6%)
    pallas_call x1, Pallas kernels, per_device(): pl.pallas_call(functools.partial(kernel, mesh_size), out_shape=jax.ShapeD...  67.9 us
    unnamed x7, local copies, waits for them, and re-layouts  4.31 us

profile of v1, /device:TPU:8, one launch (start us, length us, event | category | flops | bytes accessed | tf_op | source)
XLA Modules:
  0.0 72.2 jit_solution(1016265293981712792)
XLA Ops:
  0.0 0.0 copy-start
  0.0 1.6 %copy-done = f32[8,16,32,128]{3,2,1,0:T(8,128)S(1)} copy-done((f32[8,16,32,128]{3,2,1,0:T(8,128)S(1)}, f32[8,16,32,128]{3,2,1,0:T(8,128)}, u32[]{:S(2)}) %copy-start) | copy-done | bytes 2097176
  1.6 0.0 copy-start.1
  1.6 0.7 copy-done.1
  2.3 0.0 copy-start.2
  2.3 0.7 copy-done.2
  3.0 67.9 %shard_map.37 = f32[8,16,32,128]{3,2,1,0:T(8,128)S(1)} custom-call(f32[8,16,32,128]{3,2,1,0:T(8,128)S(1)} %copy-done, s32[16,32]{1,0:T(8,128)S(1)} %copy-done.2, f32[3,8,8]{2,1,0:T(8,128)S(1)} %copy-done.1), custom_call_target="tpu_custom_call" | custom-call | tf_op jit(solution)/shard_map/pallas_call | solution.py:385
  70.9 1.3 %copy.5 = f32[8,16,32,128]{3,2,1,0:T(8,128)} copy(f32[8,16,32,128]{3,2,1,0:T(8,128)S(1)} %shard_map.37) | data formatting | bytes 4194304
Async XLA Ops:
  0.0 1.6 %copy-start = (f32[8,16,32,128]{3,2,1,0:T(8,128)S(1)}, f32[8,16,32,128]{3,2,1,0:T(8,128)}, u32[]{:S(2)}) copy-start(f32[8,16,32,128]{3,2,1,0:T(8,128)} %state_ref.1) | copy-start | bytes 6291460
  1.6 0.7 copy-start.1
  2.3 0.7 copy-start.2

commit v2 on v1

v2 whole, which is shorter than its diff:
```python
import functools

import jax
import jax.numpy as jnp
from jax import lax
from jax.experimental import pallas as pl
from jax.experimental.pallas import tpu as pltpu
from jax.sharding import PartitionSpec as P

MESH = pl.DeviceIdType.MESH
ITERS = 3
EDGE = 8
X_CHIPS = 4
LAG = 8
QUARTERS = 3
HAND_ON = tuple((0, p, 0, 0) for p in range(QUARTERS)) + ((1, 0, 0, 3), (1, 1, 0, 4), (1, 2, 0, 5), (2, 0, 1, 7), (2, 1, 2, 0), (2, 2, 2, 1))

time_step = 0.25
lateral_mix = 0.05
vertical_mix = 0.1
pressure_scale = 0.05
thermal_coef = 1.0
haline_coef = 0.8
coriolis_mean = 0.5
coriolis_slope = 0.5


def weights(speed, scale):
    size = jnp.abs(speed)
    mix = scale * lateral_mix
    eight = speed * (scale * 8.0 / 12.0)
    four = size * (scale * 4.0 / 12.0) + mix
    return four - eight, four + eight, (speed - size) * (scale / 12.0), (speed + size) * (-scale / 12.0)


def halves(value):
    high = value.astype(jnp.bfloat16)
    return high, (value - high.astype(jnp.float32)).astype(jnp.bfloat16)


def kernel(
    mesh_size, state_ref, levels_ref, reaction_ref, out_ref, pad0, pad1, pad2, vel, mask, level, mixing, rates, summing, slope,
    push, detour, coupling, load_sem, vel_send, vel_recv, x_send, x_recv, y_send, y_recv, detour_recv, detour_send,
):
    count_gx, count_gy = mesh_size
    pads = (pad0, pad1, pad2)
    fields, rows, cells_y, depth = state_ref.shape
    pairs = rows // 2
    tiles = cells_y // 8
    slot = lax.axis_index("comp")
    gx = lax.axis_index("gx")
    gy = lax.axis_index("gy")

    def along(by):
        return {"gx": lax.rem(gx + (count_gx + by), count_gx)}

    east, west = along(1), along(-1)
    south = {"gy": lax.rem(gy + 1, count_gy)}
    north = {"gy": lax.rem(gy + count_gy - 1, count_gy)}
    chip = lax.rem(gx, X_CHIPS)
    first_chip, last_chip = chip == 0, chip == X_CHIPS - 1
    inside = pl.ds(EDGE, cells_y)

    def load(j, first, size):
        return pltpu.make_async_copy(
            state_ref.at[:, pl.ds(first, size)], pad0.at[:, pl.ds(2 + first, size), inside], load_sem.at[j]
        )

    loads = [load(0, 0, 2), load(1, rows - 2, 2), load(2, 2, rows - 4)]
    small = [
        pltpu.make_async_copy(levels_ref, level, load_sem.at[3]),
        pltpu.make_async_copy(reaction_ref, coupling, load_sem.at[4]),
    ]
    for copy in small + loads:
        copy.start()

    barrier = pltpu.get_barrier_semaphore()
    nearby = [along(by) for by in (1, -1, X_CHIPS, -X_CHIPS, X_CHIPS - 1, 1 - X_CHIPS)]
    nearby += [south, north, {"comp": lax.rem(slot + 1, 4)}, {"comp": lax.rem(slot + 3, 4)}]
    for near in nearby:
        pl.semaphore_signal(barrier, inc=1, device_id=near, device_id_type=MESH)

    lane = lax.broadcasted_iota(jnp.int32, (8, depth), 1)
    own_y = lax.broadcasted_iota(jnp.int32, (8, cells_y), 0)
    at_y = lax.broadcasted_iota(jnp.int32, (8, cells_y), 1)
    lanes = lane.astype(jnp.float32)
    def set_mask(row):
        here = jnp.broadcast_to(level[pl.ds(row, 1), :], (8, cells_y)).astype(jnp.float32)
        for t in range(tiles):
            column = jnp.sum(jnp.where(at_y == own_y + 8 * t, here, 0.0), axis=1, keepdims=True)
            mask[row, pl.ds(8 * t, 8)] = jnp.where(lanes < column, 1.0, 0.0)

    for copy in small:
        copy.wait()
    for row in (0, rows - 1, 1, rows - 2):
        set_mask(row)

    def wall(first):
        zeros = jnp.zeros((8, depth), jnp.float32)

        @pl.loop(0, rows)
        def _(row):
            for pad in pads:
                for f in range(fields):
                    pad[f, 2 + row, pl.ds(first, 8)] = zeros

    def neighbours_above_below(scale):
        up = jnp.where(lane > 0, scale, 0.0)
        down = jnp.where(lane < depth - 1, scale, 0.0)
        return lambda q: up * pltpu.roll(q, 1, 1) + down * pltpu.roll(q, depth - 1, 1)

    def cover(row):
        for f in range(fields):
            pad0[f, 2 + row, inside] = pad0[f, 2 + row, inside] * mask[row]

    def remote(source, target, send, recv, to):
        return pltpu.make_async_remote_copy(
            src_ref=source, dst_ref=target, send_sem=send, recv_sem=recv, device_id=to, device_id_type=MESH
        )

    def piece(p, kinds):
        return pl.ds(p * (kinds // 4), kinds // 4)

    def send_x(step, j, kinds):
        pad = pads[step]
        for side, row, to_row, to, turns, by in (
            (0, j, rows + j, west, first_chip, X_CHIPS - 1),
            (1, rows - 1 - j, -1 - j, east, last_chip, 1 - X_CHIPS),
        ):

            def straight():
                remote(
                    pad.at[pl.ds(0, kinds), 2 + row, inside],
                    pad.at[pl.ds(0, kinds), 2 + to_row, inside],
                    x_send.at[step, side, j],
                    x_recv.at[step, side, j],
                    to,
                ).start()

            def round_about():
                for p in range(4):
                    if p < QUARTERS:
                        target, recv, device = detour.at[step, piece(p, kinds)], detour_recv.at[step, p], along(by)
                    else:
                        target, recv, device = pad.at[piece(p, kinds), 2 + to_row, inside], x_recv.at[step, side, j], to
                    remote(pad.at[piece(p, kinds), 2 + row, inside], target, x_send.at[step, side, j], recv, device).start()

            away = turns & (j == 0)
            pl.when(away)(round_about)
            pl.when(jnp.logical_not(away))(straight)

    def detour_copies(step, kinds):
        pad = pads[step]
        for here, side, to_row, by in ((first_chip, 1, -1, X_CHIPS), (last_chip, 0, rows, -X_CHIPS)):
            for p in range(QUARTERS):
                yield p, here, remote(
                    detour.at[step, piece(p, kinds)],
                    pad.at[piece(p, kinds), 2 + to_row, inside],
                    detour_send.at[step, p],
                    x_recv.at[step, side, 0],
                    along(by),
                ), remote(
                    detour.at[step, piece(p, kinds)],
                    detour.at[step, piece(p, kinds)],
                    detour_send.at[step, p],
                    detour_recv.at[step, p],
                    along(by),
                )

    def pass_on(step, wanted, kinds):
        for p, here, onward, arriving in detour_copies(step, kinds):
            if p == wanted:

                @pl.when(here)
                def _():
                    arriving.wait_recv()
                    onward.start()

    def end_x(step, j, kinds, sent):
        for side in range(2):
            block = pads[step].at[pl.ds(0, kinds), 2, inside]
            copy = remote(block, block, x_send.at[step, side, j], x_recv.at[step, side, j], east)
            copy.wait_send() if sent else copy.wait_recv()

    def y_copies(step, j, kinds):
        for group in (j, pairs - 1 - j):
            at = pl.ds(2 + 2 * group, 2)
            for side, first, to_first, to in ((0, EDGE, EDGE + cells_y, north), (1, EDGE + cells_y - 2, EDGE - 2, south)):
                yield side, remote(
                    pads[step].at[pl.ds(0, kinds), at, pl.ds(first, 2)],
                    pads[step].at[pl.ds(0, kinds), at, pl.ds(to_first, 2)],
                    y_send.at[step, side, group],
                    y_recv.at[step, side, group],
                    to,
                )

    def send_y(step, j, kinds):
        for side, copy in y_copies(step, j, kinds):
            pl.when(gy > 0 if side == 0 else gy < count_gy - 1)(copy.start)

    def end_y(step, j, kinds, sent):
        for side, copy in y_copies(step, j, kinds):
            if sent:
                pl.when(gy > 0 if side == 0 else gy < count_gy - 1)(copy.wait_send)
            else:
                pl.when(gy < count_gy - 1 if side == 0 else gy > 0)(copy.wait_recv)

    def vel_copy(step, row, source, to):
        return remote(source, vel.at[step, :, row], vel_send.at[step, row], vel_recv.at[step, row], {"comp": to})

    def send_vel(step, k):
        for row, to in ((k, 1), (rows - 1 - k, 3)):
            vel_copy(step, row, pads[step].at[pl.ds(0, 3), 2 + row, inside], to).start()

    def start(kinds, feeds):
        for j in range(2):
            loads[j].wait()
        for row in (0, rows - 1, 1, rows - 2):
            cover(row)
        pl.semaphore_wait(barrier, len(nearby))
        for j in range(2):
            send_x(0, j, kinds)
        if feeds:

            @pl.loop(0, pairs)
            def _(k):
                for row, to in ((k, 1), (rows - 1 - k, 3)):
                    vel_copy(0, row, state_ref.at[pl.ds(0, 3), row], to).start()

        send_y(0, 0, kinds)
        pl.when(gy == 0)(lambda: wall(0))
        pl.when(gy == count_gy - 1)(lambda: wall(EDGE + cells_y))
        loads[2].wait()

        @pl.loop(1, pairs // 2)
        def _(j):
            for k in (2 * j, 2 * j + 1):
                for row in (k, rows - 1 - k):
                    set_mask(row)
                    cover(row)
            send_y(0, j, kinds)

    def each_pair(kinds, first_pair, hand_on, compute, after):
        for step in range(ITERS):

            @pl.loop(0, pairs)
            def _(i):
                k = lax.rem(i + first_pair[step], pairs)
                odd = lax.rem(k, 2)

                for ready, p, at, when in hand_on:
                    if at == step:
                        pl.when(i == when)(lambda: pass_on(ready, p, kinds))

                @pl.when(k == 0)
                def _():
                    for j in range(2):
                        end_x(step, j, kinds, False)

                @pl.when(odd == 0)
                def _():
                    end_y(step, k // 2, kinds, False)

                compute(step, i, k)
                if step < ITERS - 1:
                    after(step + 1, k)
                    pl.when(k < 2)(lambda: send_x(step + 1, k, kinds))
                    pl.when(odd == 1)(lambda: send_y(step + 1, k // 2, kinds))

        for step in range(ITERS):
            for j in range(2):
                end_x(step, j, kinds, True)

            @pl.loop(0, pairs // 2)
            def _(j):
                end_y(step, j, kinds, True)

            for _, here, onward, _ in detour_copies(step, kinds):
                pl.when(here)(onward.wait_send)

    def cell(step, f, x, t, shift=0):
        return pads[step][f, x, pl.ds(EDGE + 8 * t + shift, 8)]

    def put(step, f, row, t, value):
        if step < ITERS:
            pads[step][f, 2 + row, pl.ds(EDGE + 8 * t, 8)] = value
        else:
            out_ref[f, row, pl.ds(8 * t, 8)] = value

    def density_slopes(step, row, at):
        x = row + 2
        scale = pressure_scale / 12.0

        def difference(f, t, along_x):
            if along_x:
                one, two = cell(step, f, x + 1, t) - cell(step, f, x - 1, t), cell(step, f, x + 2, t) - cell(step, f, x - 2, t)
            else:
                one, two = cell(step, f, x, t, 1) - cell(step, f, x, t, -1), cell(step, f, x, t, 2) - cell(step, f, x, t, -2)
            return 8.0 * one - two

        for t in range(tiles):
            for way, along_x in enumerate((True, False)):
                salt, heat = difference(3, t, along_x), difference(2, t, along_x)
                slope[pl.ds(at + (way * tiles + t) * 8, 8)] = (scale * haline_coef) * salt - (scale * thermal_coef) * heat

    def dynamics_row(step, row, at, beside):
        x = row + 2
        for t in range(tiles):
            u, v = cell(step, 0, x, t), cell(step, 1, x, t)
            m = mask[row, pl.ds(8 * t, 8)]
            along_x, along_y = weights(u, 1.0), weights(v, 1.0)
            middle = -0.5 * (jnp.abs(u) + jnp.abs(v)) - (4.0 * lateral_mix + 2.0 * vertical_mix)
            y = gy * cells_y + 8 * t + lax.broadcasted_iota(jnp.int32, (8, depth), 0)
            latitude = 2.0 * y.astype(jnp.float32) / float(cells_y * count_gy - 1) - 1.0
            spin = coriolis_mean + coriolis_slope * latitude
            for f in (2, 3, 0, 1):
                q = cell(step, f, x, t)
                total = middle * q + beside(q)
                for w, shift in zip(along_x, (1, -1, 2, -2)):
                    total += w * cell(step, f, x + shift, t)
                for w, shift in zip(along_y, (1, -1, 2, -2)):
                    total += w * cell(step, f, x, t, shift)
                if f == 0:
                    total += spin * v - push[pl.ds(at + t * 8, 8)]
                if f == 1:
                    total -= spin * u + push[pl.ds(at + (tiles + t) * 8, 8)]
                before = cell(step, 4 + f, x, t)
                put(step + 1, f, row, t, m * (q + ((1.5 * time_step) * total - (0.5 * time_step) * before)))
                put(step + 1, 4 + f, row, t, m * total)

    def run_dynamics():
        above = lax.rem(lax.broadcasted_iota(jnp.int32, (2 * depth, depth), 0), depth)
        below = lax.broadcasted_iota(jnp.int32, (2 * depth, depth), 1)
        summing[...] = jnp.where(above <= below, 1.0, 0.0).astype(jnp.bfloat16)
        start(4, True)
        beside = neighbours_above_below(vertical_mix)

        def compute(step, i, k):
            density_slopes(step, k, 0)
            density_slopes(step, rows - 1 - k, 2 * cells_y)
            high, low = halves(slope[...])
            push[...] = jnp.dot(
                jnp.concatenate([high, low], axis=1), summing[...], preferred_element_type=jnp.float32
            )
            dynamics_row(step, k, 0, beside)
            dynamics_row(step, rows - 1 - k, 2 * cells_y, beside)

        each_pair(4, [pairs // 2] * ITERS, [(step, p, step, pairs // 2) for step in range(ITERS) for p in range(QUARTERS)], compute, send_vel)

        @pl.loop(0, ITERS)
        def _(step):
            @pl.loop(0, rows)
            def _(row):
                vel_copy(step, row, vel.at[step, :, row], 1).wait_send()

    def react(step, row, at):
        for t in range(0, tiles, 2):
            parts = []
            for tile in (t, t + 1):
                q = pads[step][:, row + 2, pl.ds(EDGE + 8 * tile, 8)].reshape(8 * fields, depth)
                high, low = halves(q)
                parts.append(jnp.concatenate([high, low, high], axis=0))
            rates[at + t // 2] = jnp.dot(
                mixing[...], jnp.concatenate(parts, axis=1), preferred_element_type=jnp.float32
            )

    def tracer_row(step, row, at, beside):
        x = row + 2
        for t in range(tiles):
            here = pl.ds(8 * t, 8)
            u, v, heat = vel[step, 0, row, here], vel[step, 1, row, here], vel[step, 2, row, here]
            m = mask[row, here]
            along_x, along_y = weights(u, time_step), weights(v, time_step)
            middle = (-0.5 * time_step) * (jnp.abs(u) + jnp.abs(v)) + (
                1.0 - time_step * (4.0 * lateral_mix + 2.0 * vertical_mix)
            )
            growth = (2.0 * time_step) * jax.nn.sigmoid(heat)
            for f in range(fields):
                q = cell(step, f, x, t)
                total = middle * q + growth * rates[at + t // 2, pl.ds(8 * f, 8), pl.ds((t % 2) * depth, depth)]
                for w, shift in zip(along_x, (1, -1, 2, -2)):
                    total += w * cell(step, f, x + shift, t)
                for w, shift in zip(along_y, (1, -1, 2, -2)):
                    total += w * cell(step, f, x, t, shift)
                total += beside(q)
                put(step + 1, f, row, t, m * total)

    def run_tracers():
        column = lax.broadcasted_iota(jnp.int32, (8, 3 * 8 * fields), 1)
        same = lax.rem(column, 8) == lax.broadcasted_iota(jnp.int32, (8, 3 * 8 * fields), 0)
        source = lax.rem(column, 8 * fields) // 8
        blocks = []
        for i in range(fields):
            block = jnp.zeros((8, 3 * 8 * fields), jnp.float32)
            for j in range(fields):
                block = jnp.where(same & (source == j), coupling[slot - 1, i, j], block)
            high = block.astype(jnp.bfloat16).astype(jnp.float32)
            blocks.append(jnp.where(column < 2 * 8 * fields, high, block - high))
        mixing[...] = jnp.concatenate(blocks, axis=0).astype(jnp.bfloat16)
        start(fields, False)
        beside = neighbours_above_below(time_step * vertical_mix)
        total = ITERS * pairs
        ahead = LAG * (3 - slot) // 2
        behind = LAG * (slot - 1) // 2

        def relay(c, up, last, to):
            step = c // pairs
            k = (c + (step + 2) // 3 * (pairs // 2)) % pairs
            row = k if up else rows - 1 - k
            copy = vel_copy(step, row, vel.at[step, :, row], to)
            copy.wait_recv()
            pl.when(last)(copy.start)

        def going_up(c):
            relay(c, True, slot < 3, lax.rem(slot + 1, 4))

        def going_down(c):
            relay(c, False, slot > 1, slot - 1)

        @pl.loop(0, ahead)
        def _(c):
            going_up(c)

        @pl.loop(0, behind)
        def _(c):
            going_down(c)

        def compute(step, i, k):
            react(step, k, 0)
            react(step, rows - 1 - k, tiles // 2)
            n = step * pairs + i
            pl.when(n + ahead < total)(lambda: going_up(n + ahead))
            tracer_row(step, k, 0, beside)
            pl.when(n + behind < total)(lambda: going_down(n + behind))
            tracer_row(step, rows - 1 - k, tiles // 2, beside)

        each_pair(fields, [0] + [pairs // 2] * (ITERS - 1), HAND_ON, compute, lambda step, k: None)

        @pl.loop(0, total)
        def _(c):
            step = c // pairs
            k = c % pairs
            pl.when(slot < 3)(lambda: vel_copy(step, k, vel.at[step, :, k], 1).wait_send())
            pl.when(slot > 1)(lambda: vel_copy(step, rows - 1 - k, vel.at[step, :, k], 1).wait_send())

    pl.when(slot == 0)(run_dynamics)
    pl.when(slot != 0)(run_tracers)


def solution(mesh):
    mesh_size = (mesh.shape["gx"], mesh.shape["gy"])

    def per_device(state, levels, reaction):
        fields, rows, cells_y, depth = state.shape
        dma = pltpu.SemaphoreType.DMA
        padded = (fields, rows + 4, cells_y + 2 * EDGE, depth)
        return pl.pallas_call(
            functools.partial(kernel, mesh_size),
            out_shape=jax.ShapeDtypeStruct(state.shape, state.dtype),
            in_specs=[pl.BlockSpec(memory_space=pltpu.HBM)] * 3,
            out_specs=pl.BlockSpec(memory_space=pltpu.VMEM),
            scratch_shapes=[
                *[pltpu.VMEM(padded, jnp.float32)] * ITERS,
                pltpu.VMEM((ITERS, 3, rows, cells_y, depth), jnp.float32),
                pltpu.VMEM((rows, cells_y, depth), jnp.float32),
                pltpu.VMEM(levels.shape, jnp.int32),
                pltpu.VMEM((8 * fields, 3 * 8 * fields), jnp.bfloat16),
                pltpu.VMEM((cells_y // 8, 8 * fields, 2 * depth), jnp.float32),
                pltpu.VMEM((2 * depth, depth), jnp.bfloat16),
                pltpu.VMEM((4 * cells_y, depth), jnp.float32),
                pltpu.VMEM((4 * cells_y, depth), jnp.float32),
                pltpu.VMEM((ITERS, fields, cells_y, depth), jnp.float32),
                pltpu.SMEM(reaction.shape, jnp.float32),
                dma((5,)),
                dma((ITERS, rows)),
                dma((ITERS, rows)),
                dma((ITERS, 2, 2)),
                dma((ITERS, 2, 2)),
                dma((ITERS, 2, rows // 2)),
                dma((ITERS, 2, rows // 2)),
                dma((ITERS, QUARTERS)),
                dma((ITERS, QUARTERS)),
            ],
            compiler_params=pltpu.CompilerParams(
                collective_id=0, has_side_effects=True, vmem_limit_bytes=40 * 1024 * 1024
            ),
        )(*[pltpu.with_memory_space_constraint(a, pltpu.HBM) for a in (state, levels, reaction)])

    in_specs = (P("comp", "gx", "gy", None), P("gx", "gy"), P())
    out_specs = P("comp", "gx", "gy", None)
    return jax.shard_map(per_device, mesh=mesh, in_specs=in_specs, out_specs=out_specs, check_vma=False)
```

time: 72.4 us -> 53.5 us (0.74)
  Pallas kernels: 67.9 us -> 52.1 us
  local copies, waits for them, and re-layouts: 4.31 us -> 1.32 us
    pallas_call x1, Pallas kernels: 67.9 us -> 52.1 us  [per_device(): pl.pallas_call(functools.partial(kernel, mesh_size), out_shape=jax.ShapeD...]
    unnamed x7 -> x1, local copies, waits for them, and re-layouts: 4.31 us -> 1.32 us
where the time goes in v2:
time: 53.5 us; the launch traced here: 53.4 us
  Pallas kernels  52.1 us (97%)
  local copies, waits for them, and re-layouts  1.32 us (2%)
    pallas_call x1, Pallas kernels, per_device(): pl.pallas_call(functools.partial(kernel, mesh_size), out_shape=jax.ShapeD...  52.1 us
    unnamed x1, local copies, waits for them, and re-layouts  1.32 us

profile of v2, /device:TPU:8, one launch (start us, length us, event | category | flops | bytes accessed | tf_op | source)
XLA Modules:
  0.0 53.4 jit_solution(1189049571578681925)
XLA Ops:
  0.0 52.1 %shard_map.37 = f32[8,16,32,128]{3,2,1,0:T(8,128)S(1)} custom-call(f32[8,16,32,128]{3,2,1,0:T(8,128)} %state_ref.1, s32[16,32]{1,0:T(8,128)} %levels_ref.1, f32[3,8,8]{2,1,0:T(8,128)} %reaction_ref.1), custom_call_target="tpu_custom_call" | custom-call | tf_op jit(solution)/shard_map/pallas_call | solution.py:457
  52.1 1.3 %copy.5 = f32[8,16,32,128]{3,2,1,0:T(8,128)} copy(f32[8,16,32,128]{3,2,1,0:T(8,128)S(1)} %shard_map.37) | data formatting | bytes 4194304

commit v3 on v2

--- a/solution.py
+++ b/solution.py
@@ -13,7 +13,7 @@
 X_CHIPS = 4
 LAG = 8
 QUARTERS = 3
-HAND_ON = tuple((0, p, 0, 0) for p in range(QUARTERS)) + ((1, 0, 0, 3), (1, 1, 0, 4), (1, 2, 0, 5), (2, 0, 1, 7), (2, 1, 2, 0), (2, 2, 2, 1))
+HAND_ON = tuple((0, p, 0, 0) for p in range(QUARTERS)) + ((1, 0, 0, 4), (1, 1, 0, 5), (1, 2, 0, 6), (2, 0, 2, 0), (2, 1, 2, 1), (2, 2, 2, 2))
 
 time_step = 0.25
 lateral_mix = 0.05
@@ -213,13 +213,12 @@
             vel_copy(step, row, pads[step].at[pl.ds(0, 3), 2 + row, inside], to).start()
 
     def start(kinds, feeds):
-        for j in range(2):
-            loads[j].wait()
-        for row in (0, rows - 1, 1, rows - 2):
-            cover(row)
+        if not feeds:
+            for j in range(2):
+                loads[j].wait()
+            for row in (0, rows - 1, 1, rows - 2):
+                cover(row)
         pl.semaphore_wait(barrier, len(nearby))
-        for j in range(2):
-            send_x(0, j, kinds)
         if feeds:
 
             @pl.loop(0, pairs)
@@ -227,6 +226,12 @@
                 for row, to in ((k, 1), (rows - 1 - k, 3)):
                     vel_copy(0, row, state_ref.at[pl.ds(0, 3), row], to).start()
 
+            for j in range(2):
+                loads[j].wait()
+            for row in (0, rows - 1, 1, rows - 2):
+                cover(row)
+        for j in range(2):
+            send_x(0, j, kinds)
         send_y(0, 0, kinds)
         pl.when(gy == 0)(lambda: wall(0))
         pl.when(gy == count_gy - 1)(lambda: wall(EDGE + cells_y))
@@ -240,13 +245,24 @@
                     cover(row)
             send_y(0, j, kinds)
 
-    def each_pair(kinds, first_pair, hand_on, compute, after):
+    def order(kind, i):
+        half = pairs // 4
+        group = i // 2
+        late = group // half
+        inwards = group
+        middle = (group + half) % (2 * half)
+        outwards = (1 - late) * (group + half) + late * (2 * half - 1 - group)
+        chosen = (1 - kind) * (2 - kind) // 2 * inwards + kind * (2 - kind) * middle + kind * (kind - 1) // 2 * outwards
+        return 2 * chosen + i % 2
+
+    def each_pair(kinds, orders, hand_on, prepare, compute, after):
         for step in range(ITERS):
 
             @pl.loop(0, pairs)
             def _(i):
-                k = lax.rem(i + first_pair[step], pairs)
+                k = order(orders[step], i)
                 odd = lax.rem(k, 2)
+                prepare(step, k)
 
                 for ready, p, at, when in hand_on:
                     if at == step:
@@ -345,7 +361,7 @@
             dynamics_row(step, k, 0, beside)
             dynamics_row(step, rows - 1 - k, 2 * cells_y, beside)
 
-        each_pair(4, [pairs // 2] * ITERS, [(step, p, step, pairs // 2) for step in range(ITERS) for p in range(QUARTERS)], compute, send_vel)
+        each_pair(4, [1, 2, 2], [(step, p, step, (4, 6, 6)[step]) for step in range(ITERS) for p in range(QUARTERS)], lambda step, k: None, compute, send_vel)
 
         @pl.loop(0, ITERS)
         def _(step):
@@ -386,6 +402,7 @@
                 put(step + 1, f, row, t, m * total)
 
     def run_tracers():
+        start(fields, False)
         column = lax.broadcasted_iota(jnp.int32, (8, 3 * 8 * fields), 1)
         same = lax.rem(column, 8) == lax.broadcasted_iota(jnp.int32, (8, 3 * 8 * fields), 0)
         source = lax.rem(column, 8 * fields) // 8
@@ -397,7 +414,6 @@
             high = block.astype(jnp.bfloat16).astype(jnp.float32)
             blocks.append(jnp.where(column < 2 * 8 * fields, high, block - high))
         mixing[...] = jnp.concatenate(blocks, axis=0).astype(jnp.bfloat16)
-        start(fields, False)
         beside = neighbours_above_below(time_step * vertical_mix)
         total = ITERS * pairs
         ahead = LAG * (3 - slot) // 2
@@ -405,7 +421,7 @@
 
         def relay(c, up, last, to):
             step = c // pairs
-            k = (c + (step + 2) // 3 * (pairs // 2)) % pairs
+            k = order(step, c % pairs)
             row = k if up else rows - 1 - k
             copy = vel_copy(step, row, vel.at[step, :, row], to)
             copy.wait_recv()
@@ -425,16 +441,18 @@
         def _(c):
             going_down(c)
 
-        def compute(step, i, k):
+        def prepare(step, k):
             react(step, k, 0)
             react(step, rows - 1 - k, tiles // 2)
+
+        def compute(step, i, k):
             n = step * pairs + i
             pl.when(n + ahead < total)(lambda: going_up(n + ahead))
             tracer_row(step, k, 0, beside)
             pl.when(n + behind < total)(lambda: going_down(n + behind))
             tracer_row(step, rows - 1 - k, tiles // 2, beside)
 
-        each_pair(fields, [0] + [pairs // 2] * (ITERS - 1), HAND_ON, compute, lambda step, k: None)
+        each_pair(fields, [0, 1, 2], HAND_ON, prepare, compute, lambda step, k: None)
 
         @pl.loop(0, total)
         def _(c):

time: 53.5 us -> 51.8 us (0.968)
  Pallas kernels: 52.1 us -> 50.3 us
    pallas_call x1, Pallas kernels: 52.1 us -> 50.3 us  [per_device(): pl.pallas_call(functools.partial(kernel, mesh_size), out_shape=jax.ShapeD...]
where the time goes in v3:
time: 51.8 us; the launch traced here: 51.6 us
  Pallas kernels  50.3 us (97%)
  local copies, waits for them, and re-layouts  1.32 us (3%)
    pallas_call x1, Pallas kernels, per_device(): pl.pallas_call(functools.partial(kernel, mesh_size), out_shape=jax.ShapeD...  50.3 us
    unnamed x1, local copies, waits for them, and re-layouts  1.32 us

profile of v3, /device:TPU:8, one launch (start us, length us, event | category | flops | bytes accessed | tf_op | source)
XLA Modules:
  0.0 51.6 jit_solution(14786232966475439724)
XLA Ops:
  0.0 50.3 %shard_map.37 = f32[8,16,32,128]{3,2,1,0:T(8,128)S(1)} custom-call(f32[8,16,32,128]{3,2,1,0:T(8,128)} %state_ref.1, s32[16,32]{1,0:T(8,128)} %levels_ref.1, f32[3,8,8]{2,1,0:T(8,128)} %reaction_ref.1), custom_call_target="tpu_custom_call" | custom-call | tf_op jit(solution)/shard_map/pallas_call | solution.py:475
  50.3 1.3 %copy.5 = f32[8,16,32,128]{3,2,1,0:T(8,128)} copy(f32[8,16,32,128]{3,2,1,0:T(8,128)S(1)} %shard_map.37) | data formatting | bytes 4194304
